TPU v7x, 32 devices: a whole 2x2x4 slice. The times are simulated.
32 devices in a mesh: blk: 16 (over z, y, x), grp: 2 (over core).
Axes of the slice: x: 2, y: 2, z: 4, core: 2. Of those that a mesh axis runs over, the one named last changes fastest.
Arguments:
- schur_blocks: bfloat16 [64, 1024, 1024], P(('blk', 'grp')), may hold values from -1 to 5, as said below
- residual: float32 [64, 1024, 128], P(('blk', 'grp')), may hold values from -200 to 200
- direction: float32 [64, 1024, 128], P(('blk', 'grp')), may hold values from -200 to 200
- corner_map: int32 [64, 24], P(('blk', 'grp')), may hold values from 0 to 511
- panel_order: int32 [8], replicated, may hold values from 0 to 7, each once
- coarse_factor: float32 [8, 8, 1024, 1024], P(None, None, 'blk'), may hold values from -0.0625 to 0.0625
- block_inverses: float32 [8, 1024, 1024], P(None, 'blk'), may hold values from -0.1875 to 0.1875
Outputs:
- residual_next: float32 [64, 1024, 128], P(('blk', 'grp'))
- direction_next: float32 [64, 1024, 128], P(('blk', 'grp'))
Inputs may be any that keep to these rules, and one draw needn't show every extreme that they name: `schur_blocks`: each subdomain's block is symmetric positive definite. `panel_order`: each coarse block appears once.
All inputs are finite; a program needn't handle non-finite values.
Results may differ from a plain program's by a relative error of at most 0.0048.
Values sent between devices are 32-bit elements; how exact they have to be, the bound alone decides.
No kernel may reach another device: no remote copies, remote signals or barrier semaphores. Data moves between devices by JAX's collectives and lax.ppermute only.
A program may use at most 64 MiB of HBM per device.

v0:
```python
import jax
import jax.numpy as jnp
from jax import lax
from jax.sharding import PartitionSpec as P

PANELS = 8
precise = lax.Precision.HIGHEST


def squares(residual):
    return lax.psum(jnp.sum(residual * residual, axis=(0, 1)), ("blk", "grp"))


def solve(coarse, panel_order, coarse_factor, block_inverses):
    pending = jnp.zeros_like(coarse)
    solved = jnp.zeros_like(coarse)
    for position in range(PANELS):
        current = panel_order[position]
        target = lax.dynamic_index_in_dim(coarse - pending, current, 0, keepdims=False)
        inverse = lax.dynamic_index_in_dim(block_inverses, current, 0, keepdims=False)
        block_value = jnp.dot(
            inverse,
            lax.all_gather(target, "blk", axis=0, tiled=True),
            precision=precise,
            preferred_element_type=jnp.float32,
        )
        solved = lax.dynamic_update_index_in_dim(solved, block_value, current, 0)
        if position + 1 < PANELS:
            coupling = lax.dynamic_index_in_dim(coarse_factor, current, 1, keepdims=False)
            pending = pending + jnp.einsum(
                "aic,cv->aiv",
                coupling,
                lax.all_gather(block_value, "blk", axis=0, tiled=True),
                precision=precise,
            )
    return solved


def local(
    schur_blocks, residual, direction, corner_map, panel_order, coarse_factor, block_inverses
):
    panels = block_inverses.shape[0]
    rows_b = block_inverses.shape[1]
    sub_count = schur_blocks.shape[0]
    corners = corner_map.shape[1]
    columns_iota = lax.broadcasted_iota(jnp.int32, (sub_count, corners, panels * rows_b), 2)
    placing = (corner_map[:, :, None] == columns_iota).astype(jnp.float32)
    norm_now = squares(residual)
    applied = jnp.einsum(
        "sij,sjv->siv",
        schur_blocks,
        direction.astype(jnp.bfloat16),
        preferred_element_type=jnp.float32,
    )
    curvature = lax.psum(jnp.sum(direction * applied, axis=(0, 1)), ("blk", "grp"))
    step_size = norm_now / curvature
    residual = residual - step_size * applied
    norm_next = squares(residual)
    corner_part = jnp.einsum("scm,scv->mv", placing, residual[:, :corners, :], precision=precise)
    corner_part = corner_part.reshape(panels, rows_b, -1)
    coarse_part = lax.psum(corner_part, "grp")
    solved = solve(coarse_part, panel_order, coarse_factor, block_inverses)
    flat_solved = solved.reshape(panels * rows_b, -1)
    correction = jnp.einsum("scm,mv->scv", placing, flat_solved, precision=precise)
    corrected = jnp.concatenate(
        [residual[:, :corners, :] + correction, residual[:, corners:, :]], axis=1
    )
    direction = corrected + norm_next / norm_now * direction
    return (residual, direction)


def solution(mesh):
    in_specs = (
        P(("blk", "grp"), None, None),
        P(("blk", "grp"), None, None),
        P(("blk", "grp"), None, None),
        P(("blk", "grp"), None),
        P(),
        P(None, None, "blk", None),
        P(None, "blk", None),
    )
    out_specs = (P(("blk", "grp"), None, None), P(("blk", "grp"), None, None))
    return jax.shard_map(local, mesh=mesh, in_specs=in_specs, out_specs=out_specs, check_vma=False)
```

profile of v0, /device:TPU:0, one launch (start us, length us, event | category | flops | bytes accessed | tf_op | source)
XLA Modules:
  0.0 743.4 jit_solution(7819238958384494164)
XLA Ops:
  8.9 5.0 multiply_reduce_fusion.1
  13.9 41.9 %all-reduce = (f32[128]{0:T(128)S(1)}, f32[128]{0:T(128)S(1)}) all-reduce(f32[128]{0:T(128)S(1)} %multiply_reduce_fusion.2, f32[128]{0:T(128)S(1)} %get-tuple-element.14), channel_id=1, replica_groups=mesh['blk'=16,'grp'=2] {'blk','grp'}, use_global_device_ids=true, to_apply=%region_1.0 | all-reduce | flops 256 | bytes 2048 | tf_op jit(solution)/shard_map/psum | solution.py:11
  55.8 1.8 multiply_reduce_fusion
  70.6 40.0 %psum.31 = f32[128]{0:T(128)S(1)} all-reduce(f32[128]{0:T(128)S(1)} %get-tuple-element.4), channel_id=1, replica_groups=mesh['blk'=16,'grp'=2] {'blk','grp'}, use_global_device_ids=true, to_apply=%region_6.0 | all-reduce | flops 128 | bytes 1024 | tf_op jit(solution)/shard_map/psum | solution.py:11
  116.4 43.7 %all-gather = f32[1,1024,128]{2,1,0:T(8,128)S(1)} all-gather(f32[1,64,128]{2,1,0:T(8,128)S(1)} %constant_dynamic-slice_fusion), channel_id=2, replica_groups=mesh['blk'=16,'grp'=2] {'blk'}, dimensions={1}, use_global_device_ids=true | all-gather | bytes 557056 | tf_op jit(solution)/shard_map/all_gather | solution.py:23
  160.7 38.5 %all_gather.46 = f32[1024,128]{1,0:T(8,128)S(1)} all-gather(f32[64,128]{1,0:T(8,128)S(1)} %get-tuple-element.17), channel_id=1, replica_groups=mesh['blk'=16,'grp'=2] {'blk'}, dimensions={0}, use_global_device_ids=true | all-gather | bytes 557056 | tf_op jit(solution)/shard_map/all_gather | solution.py:33
  199.2 3.4 fusion.12
  202.6 40.7 %all-gather.1 = f32[1,1024,128]{2,1,0:T(8,128)S(1)} all-gather(f32[1,64,128]{2,1,0:T(8,128)S(1)} %dynamic-slice_subtract_fusion.6), channel_id=3, replica_groups=mesh['blk'=16,'grp'=2] {'blk'}, dimensions={1}, use_global_device_ids=true | all-gather | bytes 557056 | tf_op jit(solution)/shard_map/all_gather | solution.py:23
  243.8 38.6 %all_gather.48 = f32[1024,128]{1,0:T(8,128)S(1)} all-gather(f32[64,128]{1,0:T(8,128)S(1)} %get-tuple-element.19), channel_id=1, replica_groups=mesh['blk'=16,'grp'=2] {'blk'}, dimensions={0}, use_global_device_ids=true | all-gather | bytes 557056 | tf_op jit(solution)/shard_map/all_gather | solution.py:33
  282.4 3.4 fusion.21
  285.8 40.3 %all-gather.2 = f32[1,1024,128]{2,1,0:T(8,128)S(1)} all-gather(f32[1,64,128]{2,1,0:T(8,128)S(1)} %dynamic-slice_subtract_fusion.5), channel_id=4, replica_groups=mesh['blk'=16,'grp'=2] {'blk'}, dimensions={1}, use_global_device_ids=true | all-gather | bytes 557056 | tf_op jit(solution)/shard_map/all_gather | solution.py:23
  326.6 38.6 %all_gather.50 = f32[1024,128]{1,0:T(8,128)S(1)} all-gather(f32[64,128]{1,0:T(8,128)S(1)} %get-tuple-element.21), channel_id=1, replica_groups=mesh['blk'=16,'grp'=2] {'blk'}, dimensions={0}, use_global_device_ids=true | all-gather | bytes 557056 | tf_op jit(solution)/shard_map/all_gather | solution.py:33
  365.2 3.4 fusion.24
  368.6 41.1 %all-gather.3 = f32[1,1024,128]{2,1,0:T(8,128)S(1)} all-gather(f32[1,64,128]{2,1,0:T(8,128)S(1)} %dynamic-slice_subtract_fusion.4), channel_id=5, replica_groups=mesh['blk'=16,'grp'=2] {'blk'}, dimensions={1}, use_global_device_ids=true | all-gather | bytes 557056 | tf_op jit(solution)/shard_map/all_gather | solution.py:23
  410.2 38.3 %all_gather.52 = f32[1024,128]{1,0:T(8,128)S(1)} all-gather(f32[64,128]{1,0:T(8,128)S(1)} %get-tuple-element.23), channel_id=1, replica_groups=mesh['blk'=16,'grp'=2] {'blk'}, dimensions={0}, use_global_device_ids=true | all-gather | bytes 557056 | tf_op jit(solution)/shard_map/all_gather | solution.py:33
  450.3 40.8 %all-gather.4 = f32[1,1024,128]{2,1,0:T(8,128)S(1)} all-gather(f32[1,64,128]{2,1,0:T(8,128)S(1)} %dynamic-slice_subtract_fusion.3), channel_id=6, replica_groups=mesh['blk'=16,'grp'=2] {'blk'}, dimensions={1}, use_global_device_ids=true | all-gather | bytes 557056 | tf_op jit(solution)/shard_map/all_gather | solution.py:23
  491.6 38.6 %all_gather.54 = f32[1024,128]{1,0:T(8,128)S(1)} all-gather(f32[64,128]{1,0:T(8,128)S(1)} %get-tuple-element.25), channel_id=1, replica_groups=mesh['blk'=16,'grp'=2] {'blk'}, dimensions={0}, use_global_device_ids=true | all-gather | bytes 557056 | tf_op jit(solution)/shard_map/all_gather | solution.py:33
  530.2 1.8 fusion.30
  532.0 40.5 %all-gather.5 = f32[1,1024,128]{2,1,0:T(8,128)S(1)} all-gather(f32[1,64,128]{2,1,0:T(8,128)S(1)} %dynamic-slice_subtract_fusion.2), channel_id=7, replica_groups=mesh['blk'=16,'grp'=2] {'blk'}, dimensions={1}, use_global_device_ids=true | all-gather | bytes 557056 | tf_op jit(solution)/shard_map/all_gather | solution.py:23
  573.0 38.5 %all_gather.56 = f32[1024,128]{1,0:T(8,128)S(1)} all-gather(f32[64,128]{1,0:T(8,128)S(1)} %get-tuple-element.27), channel_id=1, replica_groups=mesh['blk'=16,'grp'=2] {'blk'}, dimensions={0}, use_global_device_ids=true | all-gather | bytes 557056 | tf_op jit(solution)/shard_map/all_gather | solution.py:33
  613.3 40.4 %all-gather.6 = f32[1,1024,128]{2,1,0:T(8,128)S(1)} all-gather(f32[1,64,128]{2,1,0:T(8,128)S(1)} %dynamic-slice_subtract_fusion.1), channel_id=8, replica_groups=mesh['blk'=16,'grp'=2] {'blk'}, dimensions={1}, use_global_device_ids=true | all-gather | bytes 557056 | tf_op jit(solution)/shard_map/all_gather | solution.py:23
  654.1 38.3 %all_gather.58 = f32[1024,128]{1,0:T(8,128)S(1)} all-gather(f32[64,128]{1,0:T(8,128)S(1)} %get-tuple-element.29), channel_id=1, replica_groups=mesh['blk'=16,'grp'=2] {'blk'}, dimensions={0}, use_global_device_ids=true | all-gather | bytes 557056 | tf_op jit(solution)/shard_map/all_gather | solution.py:33
  692.4 1.8 fusion
  694.2 40.5 %all-gather.7 = f32[1,1024,128]{2,1,0:T(8,128)S(1)} all-gather(f32[1,64,128]{2,1,0:T(8,128)S(1)} %dynamic-slice_subtract_fusion), channel_id=9, replica_groups=mesh['blk'=16,'grp'=2] {'blk'}, dimensions={1}, use_global_device_ids=true | all-gather | bytes 557056 | tf_op jit(solution)/shard_map/all_gather | solution.py:23
  (46 shorter events, 14.0 us)
Async XLA Ops:
  7.2 153.0 %copy-start = (f32[8,64,1024]{2,1,0:T(8,128)S(1)}, f32[8,64,1024]{2,1,0:T(8,128)}, u32[]{:S(2)}) copy-start(f32[8,64,1024]{2,1,0:T(8,128)} %param.13) | copy-start | bytes 6291460
  7.2 108.5 %all-reduce.3.cloned.1.call-start = ((), (), s32[]{:S(2)}) async-start(), calls=%async_computation | async-start | bytes 524288 | tf_op jit(solution)/shard_map/psum | solution.py:61
  13.9 43.8 %copy-start.7 = (s32[2,24]{1,0:T(2,128)S(1)}, s32[2,24]{1,0:T(2,128)}, u32[]{:S(2)}) copy-start(s32[2,24]{1,0:T(2,128)} %param.10) | copy-start | bytes 580
  13.9 45.0 %copy-start.6 = (s32[8]{0:T(128)S(1)}, s32[8]{0:T(128)}, u32[]{:S(2)}) copy-start(s32[8]{0:T(128)} %param.11) | copy-start | bytes 100
  57.6 677.5 %copy-start.2 = (f32[2,1024,128]{2,1,0:T(8,128)}, f32[2,1024,128]{2,1,0:T(8,128)S(1)}, u32[]{:S(2)}) copy-start(f32[2,1024,128]{2,1,0:T(8,128)S(1)} %get-tuple-element.5) | copy-start | bytes 3145732
  160.2 42.4 %copy-start.5 = (f32[8,64,128]{2,1,0:T(8,128)S(1)}, f32[8,64,128]{2,1,0:T(8,128)}, u32[]{:S(2)}) copy-start(f32[8,64,128]{2,1,0:T(8,128)} %all-reduce.3.cloned.1.call-done) | copy-start | bytes 786436
  160.2 288.3 %copy-start.1 = (f32[8,8,64,1024]{3,2,1,0:T(8,128)S(1)}, f32[8,8,64,1024]{3,2,1,0:T(8,128)}, u32[]{:S(2)}) copy-start(f32[8,8,64,1024]{3,2,1,0:T(8,128)} %param.12) | copy-start | bytes 50331652
  692.4 43.1 %copy-start.3 = (f32[2,1024,128]{2,1,0:T(8,128)S(1)}, f32[2,1024,128]{2,1,0:T(8,128)}, u32[]{:S(2)}) copy-start(f32[2,1024,128]{2,1,0:T(8,128)} %param.9) | copy-start | bytes 3145732
  692.4 43.1 %copy-start.4 = (f32[2,1000,128]{2,1,0:T(8,128)S(1)}, f32[2,1000,128]{2,1,0:T(8,128)}, u32[]{:S(2)}) copy-start(f32[2,1000,128]{2,1,0:T(8,128)} %slice.42) | copy-start | bytes 3072004
Sparse Core Ops, SparseCore 0:
  59.0 18.0 all-reduce.2
where the time goes:
time: 744 us; the launch traced here: 743 us
  blocking collectives  679 us (91%)
  between operations  29.3 us (4%)
  matrix products  27.4 us (4%)
    all_gather x8, blocking collectives, solve(): lax.all_gather(target, 'blk', axis=0, tiled=True)  328 us
    all_gather x7, blocking collectives, solve(): lax.all_gather(block_value, 'blk', axis=0, tiled=True)  269 us
    psum x2, blocking collectives, squares(): return lax.psum(jnp.sum(residual * residual, axis=(0, 1)), ('blk', 'grp'))  82 us
    dot_general x7, matrix products, solve(): jnp.einsum('aic,cv->aiv', coupling, lax.all_gather(block_value, 'blk', ax...  17.4 us
  transfers between devices with their start and end apart: 1, of which 0 were waited for; matrix products, arithmetic and copies ran while one was open for 0% of the time, Pallas kernels for 0%

commit v1 on v0

--- a/solution.py
+++ b/solution.py
@@ -7,8 +7,13 @@
 precise = lax.Precision.HIGHEST
 
 
+def add_all(value, axis):
+    parts = lax.all_gather(value, axis)
+    return jnp.sum(parts, axis=0)
+
+
 def squares(residual):
-    return lax.psum(jnp.sum(residual * residual, axis=(0, 1)), ("blk", "grp"))
+    return add_all(jnp.sum(residual * residual, axis=(0, 1)), ("blk", "grp"))
 
 
 def solve(coarse, panel_order, coarse_factor, block_inverses):

time: 744 us -> 778 us (1.046)
  blocking collectives: 679 us -> 713 us
    all_gather x0 -> x2, blocking collectives: none -> 83.5 us  [add_all(): parts = lax.all_gather(value, axis)]
    psum x2 -> x1, blocking collectives: 82 us -> 36.8 us  [local(): lax.psum(jnp.sum(direction * applied, axis=(0, 1)), ('blk', 'grp'))]
    all_gather x8, blocking collectives: 328 us -> 308 us  [solve(): lax.all_gather(target, 'blk', axis=0, tiled=True)]
    all_gather x7, blocking collectives: 269 us -> 285 us  [solve(): lax.all_gather(block_value, 'blk', axis=0, tiled=True)]
where the time goes in v1:
time: 778 us; the launch traced here: 777 us
  blocking collectives  713 us (92%)
  between operations  29 us (4%)
  matrix products  27.4 us (4%)
    all_gather x8, blocking collectives, solve(): lax.all_gather(target, 'blk', axis=0, tiled=True)  308 us
    all_gather x7, blocking collectives, solve(): lax.all_gather(block_value, 'blk', axis=0, tiled=True)  285 us
    all_gather x2, blocking collectives, add_all(): parts = lax.all_gather(value, axis)  83.5 us
    psum x1, blocking collectives, local(): lax.psum(jnp.sum(direction * applied, axis=(0, 1)), ('blk', 'grp'))  36.8 us
    dot_general x7, matrix products, solve(): jnp.einsum('aic,cv->aiv', coupling, lax.all_gather(block_value, 'blk', ax...  17.4 us
  transfers between devices with their start and end apart: 1, of which 0 were waited for; matrix products, arithmetic and copies ran while one was open for 0% of the time, Pallas kernels for 0%

profile of v1, /device:TPU:0, one launch (start us, length us, event | category | flops | bytes accessed | tf_op | source)
XLA Modules:
  0.0 777.2 jit_solution(5588972585734248209)
XLA Ops:
  8.9 43.3 %all-gather.10 = f32[32,1,128]{2,1,0:T(1,128)S(1)} all-gather(f32[1,1,128]{2,1,0:T(1,128)S(1)} %bitcast.167), channel_id=2, replica_groups=mesh['blk'=16,'grp'=2] {'blk','grp'}, dimensions={0}, use_global_device_ids=true | all-gather | bytes 16896 | tf_op jit(solution)/shard_map/all_gather | solution.py:11
  52.2 5.0 multiply_reduce_fusion.1
  57.2 36.8 %psum.14 = f32[128]{0:T(128)S(1)} all-reduce(f32[128]{0:T(128)S(1)} %get-tuple-element.12), channel_id=1, replica_groups=mesh['blk'=16,'grp'=2] {'blk','grp'}, use_global_device_ids=true, to_apply=%region_3.0 | all-reduce | flops 128 | bytes 1024 | tf_op jit(solution)/shard_map/psum | solution.py:60
  94.0 1.8 multiply_reduce_fusion
  108.6 40.2 %all-gather.11 = f32[32,1,128]{2,1,0:T(1,128)S(1)} all-gather(f32[1,1,128]{2,1,0:T(1,128)S(1)} %bitcast.166), channel_id=11, replica_groups=mesh['blk'=16,'grp'=2] {'blk','grp'}, dimensions={0}, use_global_device_ids=true | all-gather | bytes 16896 | tf_op jit(solution)/shard_map/all_gather | solution.py:11
  154.5 38.3 %all-gather.1 = f32[1,1024,128]{2,1,0:T(8,128)S(1)} all-gather(f32[1,64,128]{2,1,0:T(8,128)S(1)} %constant_dynamic-slice_fusion), channel_id=3, replica_groups=mesh['blk'=16,'grp'=2] {'blk'}, dimensions={1}, use_global_device_ids=true | all-gather | bytes 557056 | tf_op jit(solution)/shard_map/all_gather | solution.py:28
  193.4 41.0 %all_gather.60 = f32[1024,128]{1,0:T(8,128)S(1)} all-gather(f32[64,128]{1,0:T(8,128)S(1)} %get-tuple-element.15), channel_id=1, replica_groups=mesh['blk'=16,'grp'=2] {'blk'}, dimensions={0}, use_global_device_ids=true | all-gather | bytes 557056 | tf_op jit(solution)/shard_map/all_gather | solution.py:38
  234.4 3.4 fusion.12
  237.8 38.5 %all-gather.2 = f32[1,1024,128]{2,1,0:T(8,128)S(1)} all-gather(f32[1,64,128]{2,1,0:T(8,128)S(1)} %dynamic-slice_subtract_fusion.6), channel_id=4, replica_groups=mesh['blk'=16,'grp'=2] {'blk'}, dimensions={1}, use_global_device_ids=true | all-gather | bytes 557056 | tf_op jit(solution)/shard_map/all_gather | solution.py:28
  276.8 41.2 %all_gather.62 = f32[1024,128]{1,0:T(8,128)S(1)} all-gather(f32[64,128]{1,0:T(8,128)S(1)} %get-tuple-element.17), channel_id=1, replica_groups=mesh['blk'=16,'grp'=2] {'blk'}, dimensions={0}, use_global_device_ids=true | all-gather | bytes 557056 | tf_op jit(solution)/shard_map/all_gather | solution.py:38
  318.0 3.4 fusion.21
  321.4 38.5 %all-gather.3 = f32[1,1024,128]{2,1,0:T(8,128)S(1)} all-gather(f32[1,64,128]{2,1,0:T(8,128)S(1)} %dynamic-slice_subtract_fusion.5), channel_id=5, replica_groups=mesh['blk'=16,'grp'=2] {'blk'}, dimensions={1}, use_global_device_ids=true | all-gather | bytes 557056 | tf_op jit(solution)/shard_map/all_gather | solution.py:28
  360.4 40.4 %all_gather.64 = f32[1024,128]{1,0:T(8,128)S(1)} all-gather(f32[64,128]{1,0:T(8,128)S(1)} %get-tuple-element.19), channel_id=1, replica_groups=mesh['blk'=16,'grp'=2] {'blk'}, dimensions={0}, use_global_device_ids=true | all-gather | bytes 557056 | tf_op jit(solution)/shard_map/all_gather | solution.py:38
  400.8 3.4 fusion.24
  404.2 38.7 %all-gather.4 = f32[1,1024,128]{2,1,0:T(8,128)S(1)} all-gather(f32[1,64,128]{2,1,0:T(8,128)S(1)} %dynamic-slice_subtract_fusion.4), channel_id=6, replica_groups=mesh['blk'=16,'grp'=2] {'blk'}, dimensions={1}, use_global_device_ids=true | all-gather | bytes 557056 | tf_op jit(solution)/shard_map/all_gather | solution.py:28
  443.3 40.5 %all_gather.66 = f32[1024,128]{1,0:T(8,128)S(1)} all-gather(f32[64,128]{1,0:T(8,128)S(1)} %get-tuple-element.21), channel_id=1, replica_groups=mesh['blk'=16,'grp'=2] {'blk'}, dimensions={0}, use_global_device_ids=true | all-gather | bytes 557056 | tf_op jit(solution)/shard_map/all_gather | solution.py:38
  483.9 1.8 fusion.27
  485.7 38.6 %all-gather.5 = f32[1,1024,128]{2,1,0:T(8,128)S(1)} all-gather(f32[1,64,128]{2,1,0:T(8,128)S(1)} %dynamic-slice_subtract_fusion.3), channel_id=7, replica_groups=mesh['blk'=16,'grp'=2] {'blk'}, dimensions={1}, use_global_device_ids=true | all-gather | bytes 557056 | tf_op jit(solution)/shard_map/all_gather | solution.py:28
  524.7 40.5 %all_gather.68 = f32[1024,128]{1,0:T(8,128)S(1)} all-gather(f32[64,128]{1,0:T(8,128)S(1)} %get-tuple-element.23), channel_id=1, replica_groups=mesh['blk'=16,'grp'=2] {'blk'}, dimensions={0}, use_global_device_ids=true | all-gather | bytes 557056 | tf_op jit(solution)/shard_map/all_gather | solution.py:38
  567.0 38.9 %all-gather.6 = f32[1,1024,128]{2,1,0:T(8,128)S(1)} all-gather(f32[1,64,128]{2,1,0:T(8,128)S(1)} %dynamic-slice_subtract_fusion.2), channel_id=8, replica_groups=mesh['blk'=16,'grp'=2] {'blk'}, dimensions={1}, use_global_device_ids=true | all-gather | bytes 557056 | tf_op jit(solution)/shard_map/all_gather | solution.py:28
  606.4 41.1 %all_gather.70 = f32[1024,128]{1,0:T(8,128)S(1)} all-gather(f32[64,128]{1,0:T(8,128)S(1)} %get-tuple-element.25), channel_id=1, replica_groups=mesh['blk'=16,'grp'=2] {'blk'}, dimensions={0}, use_global_device_ids=true | all-gather | bytes 557056 | tf_op jit(solution)/shard_map/all_gather | solution.py:38
  649.2 38.3 %all-gather.7 = f32[1,1024,128]{2,1,0:T(8,128)S(1)} all-gather(f32[1,64,128]{2,1,0:T(8,128)S(1)} %dynamic-slice_subtract_fusion.1), channel_id=9, replica_groups=mesh['blk'=16,'grp'=2] {'blk'}, dimensions={1}, use_global_device_ids=true | all-gather | bytes 557056 | tf_op jit(solution)/shard_map/all_gather | solution.py:28
  688.0 40.5 %all_gather.72 = f32[1024,128]{1,0:T(8,128)S(1)} all-gather(f32[64,128]{1,0:T(8,128)S(1)} %get-tuple-element.27), channel_id=1, replica_groups=mesh['blk'=16,'grp'=2] {'blk'}, dimensions={0}, use_global_device_ids=true | all-gather | bytes 557056 | tf_op jit(solution)/shard_map/all_gather | solution.py:38
  730.3 38.3 %all-gather.8 = f32[1,1024,128]{2,1,0:T(8,128)S(1)} all-gather(f32[1,64,128]{2,1,0:T(8,128)S(1)} %dynamic-slice_subtract_fusion), channel_id=10, replica_groups=mesh['blk'=16,'grp'=2] {'blk'}, dimensions={1}, use_global_device_ids=true | all-gather | bytes 557056 | tf_op jit(solution)/shard_map/all_gather | solution.py:28
  (49 shorter events, 15.9 us)
Async XLA Ops:
  7.2 185.7 %copy-start = (f32[8,64,1024]{2,1,0:T(8,128)S(1)}, f32[8,64,1024]{2,1,0:T(8,128)}, u32[]{:S(2)}) copy-start(f32[8,64,1024]{2,1,0:T(8,128)} %param.13) | copy-start | bytes 6291460
  7.2 146.6 %all-reduce.2.cloned.1.call-start = ((), (), s32[]{:S(2)}) async-start(), calls=%async_computation | async-start | bytes 524288 | tf_op jit(solution)/shard_map/psum | solution.py:66
  57.2 38.7 %copy-start.7 = (s32[2,24]{1,0:T(2,128)S(1)}, s32[2,24]{1,0:T(2,128)}, u32[]{:S(2)}) copy-start(s32[2,24]{1,0:T(2,128)} %param.10) | copy-start | bytes 580
  57.2 39.9 %copy-start.6 = (s32[8]{0:T(128)S(1)}, s32[8]{0:T(128)}, u32[]{:S(2)}) copy-start(s32[8]{0:T(128)} %param.11) | copy-start | bytes 100
  95.9 673.2 %copy-start.2 = (f32[2,1024,128]{2,1,0:T(8,128)}, f32[2,1024,128]{2,1,0:T(8,128)S(1)}, u32[]{:S(2)}) copy-start(f32[2,1024,128]{2,1,0:T(8,128)S(1)} %get-tuple-element.3) | copy-start | bytes 3145732
  192.9 44.9 %copy-start.5 = (f32[8,64,128]{2,1,0:T(8,128)S(1)}, f32[8,64,128]{2,1,0:T(8,128)}, u32[]{:S(2)}) copy-start(f32[8,64,128]{2,1,0:T(8,128)} %all-reduce.2.cloned.1.call-done) | copy-start | bytes 786436
  192.9 290.9 %copy-start.1 = (f32[8,8,64,1024]{3,2,1,0:T(8,128)S(1)}, f32[8,8,64,1024]{3,2,1,0:T(8,128)}, u32[]{:S(2)}) copy-start(f32[8,8,64,1024]{3,2,1,0:T(8,128)} %param.12) | copy-start | bytes 50331652
  728.5 40.8 %copy-start.3 = (f32[2,1024,128]{2,1,0:T(8,128)S(1)}, f32[2,1024,128]{2,1,0:T(8,128)}, u32[]{:S(2)}) copy-start(f32[2,1024,128]{2,1,0:T(8,128)} %param.9) | copy-start | bytes 3145732
  728.5 40.8 %copy-start.4 = (f32[2,1000,128]{2,1,0:T(8,128)S(1)}, f32[2,1000,128]{2,1,0:T(8,128)}, u32[]{:S(2)}) copy-start(f32[2,1000,128]{2,1,0:T(8,128)} %slice.42) | copy-start | bytes 3072004
Sparse Core Ops, SparseCore 0:
  97.2 18.6 all-reduce.1
